TPU v7x, 32 devices: a whole 2x2x4 slice. The times are simulated.
32 devices in a mesh: groups: 2 (over y), frames: 4 (over z), heads: 4 (over x, core).
Axes of the slice: x: 2, y: 2, z: 4, core: 2. Of those that a mesh axis runs over, the one named last changes fastest.
Arguments:
- tokens: bfloat16 [64, 128, 1024], P(('groups', 'frames')), parts along dimension 0, may hold values from -12 to 12
- w_qkv: bfloat16 [1024, 3, 1024], P(None, None, 'heads'), may hold values from -1 to 1
- w_out: bfloat16 [1024, 1024], P('heads'), may hold values from -2 to 2
- pair_slots: int32 [16, 2], P(('groups', 'frames')), parts along dimension 0, may hold values from -1 to 31, as said below
Outputs:
- mixed: bfloat16 [64, 128, 1024], P(('groups', 'frames'), 'heads'), parts along dimension 0
There are 2 independent parts, one for each index of `groups`. A program takes and returns all parts, laid end to end along the dimension named above; an argument that names none is the same for every part. Nothing has to cross between parts.
Inputs may be any that keep to these rules, and one draw needn't show every extreme that they name: `pair_slots`: rows 2 * o to 2 * o + 1 are the pairs owned by device o of the frames axis, which holds frames 8 * o to 8 * o + 7. A row is two frame indices or -1 twice; in each owner's block the live rows come first, and one owner has all 2 rows live. In one owner's block no two entries of live rows belong to the same home device (frame index // 8), so a frame appears there at most once.
All inputs are finite; a program needn't handle non-finite values.
Results may differ from a plain program's by a relative error of at most 0.0081.
Values may be sent and summed in bfloat16 or wider, within the bound.
A program may use at most 64 MiB of HBM per device.

v0:
```python
import jax
import jax.numpy as jnp
from jax import lax
from jax.sharding import PartitionSpec as P

HD = 64


def attend(queries, key_rows, values):
    length, breadth = queries.shape
    head_count = breadth // HD
    query_heads = queries.reshape(length, head_count, HD)
    key_heads = key_rows.reshape(key_rows.shape[0], head_count, HD)
    value_heads = values.reshape(values.shape[0], head_count, HD)
    scores = jnp.einsum(
        "qhd,khd->hqk", query_heads, key_heads, preferred_element_type=jnp.float32
    ) * HD ** (-0.5)
    row_peak = jnp.max(scores, axis=2)
    lifted = jnp.exp(scores - row_peak[:, :, None])
    row_total = jnp.sum(lifted, axis=2)
    weighted = jnp.einsum(
        "hqk,khd->qhd", lifted.astype(jnp.bfloat16), value_heads, preferred_element_type=jnp.float32
    )
    normalized = weighted / jnp.transpose(row_total)[:, :, None]
    return (normalized.reshape(length, breadth), row_peak + jnp.log(row_total))


def local(tokens, w_qkv, w_out, pair_slots):
    frames_here, length, width_model = tokens.shape
    breadth = w_qkv.shape[2]
    head_count = breadth // HD
    devices = lax.axis_size("frames")
    position = lax.axis_index("frames")
    slots_here = pair_slots.shape[0]
    packed = jnp.dot(
        tokens.reshape(frames_here * length, width_model),
        w_qkv.reshape(width_model, 3 * breadth),
        preferred_element_type=jnp.float32,
    )
    packed = packed.astype(jnp.bfloat16).reshape(frames_here, length, 3 * breadth)
    listing = lax.all_gather(pair_slots, "frames", axis=0, tiled=True)
    first_frame = listing[:, 0]
    second_frame = listing[:, 1]
    own_frames = position * frames_here + jnp.arange(frames_here, dtype=jnp.int32)
    contains = (
        (first_frame[:, None] == own_frames[None, :])
        | (second_frame[:, None] == own_frames[None, :])
    ).astype(jnp.float32)
    owners = jnp.arange(listing.shape[0], dtype=jnp.int32) // slots_here
    owner_table = (owners[:, None] == jnp.arange(devices, dtype=jnp.int32)[None, :]).astype(
        jnp.float32
    )
    needed = jnp.dot(owner_table.T, contains)
    needed_bf = needed.astype(jnp.bfloat16)
    self_out, self_lse = jax.vmap(attend)(
        packed[:, :, :breadth], packed[:, :, breadth : 2 * breadth], packed[:, :, 2 * breadth :]
    )
    is_live = pair_slots[:, 0] >= 0
    home_first = jnp.maximum(pair_slots[:, 0], 0) // frames_here
    home_second = jnp.maximum(pair_slots[:, 1], 0) // frames_here
    outgoing = jnp.einsum(
        "of,fx->ox",
        needed_bf,
        packed.reshape(frames_here, length * 3 * breadth),
        preferred_element_type=jnp.float32,
    )
    outgoing = outgoing.astype(jnp.bfloat16).reshape(devices, length, 3 * breadth)
    arrived = lax.all_to_all(outgoing, "frames", split_axis=0, concat_axis=0, tiled=True)

    def one_pair(slot_index):
        left_block = arrived[home_first[slot_index]]
        right_block = arrived[home_second[slot_index]]
        out_left, lse_left = attend(
            left_block[:, :breadth],
            right_block[:, breadth : 2 * breadth],
            right_block[:, 2 * breadth :],
        )
        out_right, lse_right = attend(
            right_block[:, :breadth],
            left_block[:, breadth : 2 * breadth],
            left_block[:, 2 * breadth :],
        )
        return (jnp.stack([out_left, out_right]), jnp.stack([lse_left, lse_right]))

    pair_out, pair_lse = lax.map(one_pair, jnp.arange(slots_here, dtype=jnp.int32))
    targets = jnp.where(
        is_live[:, None], jnp.stack([home_first, home_second], axis=1), devices
    ).reshape(-1)
    back_out = (
        jnp.zeros((devices, length, breadth), jnp.float32)
        .at[targets]
        .set(pair_out.reshape(2 * slots_here, length, breadth), mode="drop")
    )
    back_lse = (
        jnp.zeros((devices, head_count, length), jnp.float32)
        .at[targets]
        .set(pair_lse.reshape(2 * slots_here, head_count, length), mode="drop")
    )
    got_out, got_lse = (
        lax.all_to_all(back_out, "frames", split_axis=0, concat_axis=0, tiled=True),
        lax.all_to_all(back_lse, "frames", split_axis=0, concat_axis=0, tiled=True),
    )
    needs_mask = needed > 0.5
    candidates = jnp.where(needs_mask[:, :, None, None], got_lse[:, None, :, :], -jnp.inf)
    ceiling = jnp.maximum(self_lse, jnp.max(candidates, axis=0))
    self_weight = jnp.exp(self_lse - ceiling)
    far_weight = jnp.where(needs_mask[:, :, None, None], jnp.exp(candidates - ceiling[None]), 0.0)
    weight_total = self_weight + jnp.sum(far_weight, axis=0)
    far_sum = jnp.einsum(
        "jfhl,jlhd->flhd",
        far_weight,
        got_out.reshape(devices, length, head_count, HD),
        precision=lax.Precision.HIGHEST,
    )
    merged = (
        jnp.transpose(self_weight, (0, 2, 1))[..., None]
        * self_out.reshape(frames_here, length, head_count, HD)
        + far_sum
    ) / jnp.transpose(weight_total, (0, 2, 1))[..., None]
    merged = merged.reshape(frames_here, length, breadth).astype(jnp.bfloat16)
    rows_major = jnp.transpose(merged, (1, 0, 2)).reshape(length * frames_here, breadth)
    parts_here = lax.axis_size("heads")
    projected = jnp.dot(rows_major, w_out, preferred_element_type=jnp.float32)
    own_share = lax.psum_scatter(projected, "heads", scatter_dimension=0, tiled=True)
    own_share = own_share.astype(jnp.bfloat16).reshape(
        length // parts_here, frames_here, width_model
    )
    return jnp.transpose(own_share, (1, 0, 2))


def solution(mesh):
    placed = (
        P(("groups", "frames"), None, None),
        P(None, None, "heads"),
        P("heads", None),
        P(("groups", "frames"), None),
    )
    return jax.shard_map(
        local,
        mesh=mesh,
        in_specs=placed,
        out_specs=P(("groups", "frames"), "heads", None),
        check_vma=False,
    )
```

profile of v0, /device:TPU:1, one launch (start us, length us, event | category | flops | bytes accessed | tf_op | source)
XLA Modules:
  0.0 179.7 jit_solution(4908621856031720183)
XLA Ops:
  6.5 10.3 %all-gather = s32[4,2,2]{2,1,0:T(2,128)S(1)} all-gather(s32[1,2,2]{2,1,0:T(2,128)} %bitcast.186), channel_id=1, replica_groups=mesh['groups'=2,'frames'=4,'heads'=4] {'frames'}, dimensions={0}, use_global_device_ids=true | all-gather | bytes 80 | tf_op jit(solution)/shard_map/all_gather | solution.py:41
  17.1 2.6 %copy.75 = bf16[1024,3,256]{0,2,1:T(8,128)(2,1)} copy(bf16[1024,3,256]{2,0,1:T(8,128)(2,1)} %param.7) | data formatting | bytes 3145728 | tf_op args[1]
  19.7 4.4 %convolution_convert_fusion.1 = bf16[1024,768]{1,0:T(8,128)(2,1)} fusion(bf16[1024,1024]{1,0:T(8,128)(2,1)S(1)} %bitcast.163, bf16[1024,768]{0,1:T(8,128)(2,1)} %bitcast.178), kind=kOutput, calls=%fused_computation.29 | convolution fusion | flops 1611399168 | bytes 5242880 | tf_op jit(solution)/shard_map/dot_general | solution.py:35
  24.1 3.3 %reshape_reshape.3 = bf16[8,98304]{1,0:T(8,128)(2,1)} reshape(bf16[1024,768]{1,0:T(8,128)(2,1)} %convolution_convert_fusion.1) | data formatting | bytes 3145728 | tf_op jit(solution)/shard_map/reshape;reshape | solution.py:64
  27.6 2.0 %convolution_convert_fusion = bf16[4,98304]{1,0:T(4,128)(2,1)S(1)} fusion(bf16[8,98304]{1,0:T(8,128)(2,1)} %reshape_reshape.3, bf16[4,8]{1,0:T(4,128)(2,1)S(1)} %get-tuple-element.93), kind=kOutput, calls=%fused_computation.24 | convolution fusion | flops 6684672 | bytes 2359360 | tf_op jit(solution)/shard_map/of,fx->ox/dot_general | solution.py:61
  29.7 1.2 copy.79
  30.9 3.5 %all-to-all-start = ((bf16[4,128,768]{1,2,0:T(8,128)(2,1)}), bf16[4,128,768]{1,2,0:T(8,128)(2,1)S(1)}, u32[]{:S(2)}, u32[]{:S(2)}) async-start(bf16[4,128,768]{1,2,0:T(8,128)(2,1)} %copy.79), calls=%async_computation | async-start | bytes 1572864 | tf_op jit(solution)/shard_map/all_to_all | solution.py:68
  34.9 2.5 %fusion.56 = (bf16[8,128,256]{2,1,0:T(8,128)(2,1)}, bf16[8,128,256]{2,1,0:T(8,128)(2,1)S(1)}, bf16[8,128,256]{2,1,0:T(8,128)(2,1)}) fusion(bf16[8,128,768]{2,1,0:T(8,128)(2,1)} %bitcast.168), kind=kLoop, calls=%fused_computation.100 | loop fusion | bytes 3145728 | tf_op jit(solution)/shard_map/slice | solution.py:56
  37.4 2.0 %copy.77 = bf16[8,128,256]{1,2,0:T(8,128)(2,1)} copy(bf16[8,128,256]{2,1,0:T(8,128)(2,1)} %get-tuple-element.82) | data formatting | bytes 1048576 | tf_op jit(solution)/shard_map/slice | solution.py:56
  39.5 2.0 %copy.76 = bf16[8,128,256]{1,2,0:T(8,128)(2,1)} copy(bf16[8,128,256]{2,1,0:T(8,128)(2,1)} %get-tuple-element.84) | data formatting | bytes 1048576 | tf_op jit(solution)/shard_map/slice | solution.py:56
  41.5 3.1 %multiply_reduce_fusion = (f32[8,4,128]{2,1,0:T(4,128)S(1)}, f32[8,4,128,128]{2,3,1,0:T(8,128)}) fusion(bf16[8,128,4,64]{1,3,2,0:T(8,128)(2,1)} %bitcast.175, bf16[8,128,4,64]{1,3,2,0:T(8,128)(2,1)} %bitcast.174), kind=kOutput, calls=%fused_computation.26 | convolution fusion | flops 68153344 | bytes 3162112 | tf_op jit(solution)/shard_map/vmap(qhd,khd->hqk)/dot_general | solution.py:15
  44.6 9.3 %all-to-all-done = bf16[4,128,768]{1,2,0:T(8,128)(2,1)S(1)} async-done(((bf16[4,128,768]{1,2,0:T(8,128)(2,1)}), bf16[4,128,768]{1,2,0:T(8,128)(2,1)S(1)}, u32[]{:S(2)}, u32[]{:S(2)}) %all-to-all-start) | async-done | bytes 786464 | tf_op jit(solution)/shard_map/all_to_all | solution.py:68
  53.9 19.1 %while.12 = (s32[]{:T(128)}, f32[2,2,128,256]{2,3,1,0:T(8,128)}, f32[2,2,4,128]{3,2,1,0:T(4,128)S(1)}, s32[2]{0:T(128)S(1)}, s32[2]{0:T(128)S(1)}, /*index=5*/bf...) while((s32[]{:T(128)}, f32[2,2,128,256]{2,3,1,0:T(8,128)}, ...), condition=%wide.region_7.8_spmd, body=%wide.region_2.7_spmd.sunk | while | flops 34471944 | bytes 8560967 | solution.py:85
  73.6 1.8 %scatter_fusion = f32[4,4,128]{2,1,0:T(4,128)} fusion(f32[4,4,128]{2,1,0:T(4,128)} %broadcast_in_dim.86, s32[4]{0:T(128)S(1)} %fusion.45, f32[4,4,128]{2,1,0:T(4,128)S(1)} %bitcast.187), kind=kCustom, calls=%fused_computation | custom fusion | bytes 24592 | tf_op jit(solution)/shard_map/scatter | solution.py:97
  75.4 3.2 %all-to-all-start.1 = ((f32[4,4,128]{2,1,0:T(4,128)}), f32[4,4,128]{2,1,0:T(4,128)S(1)}, u32[]{:S(2)}, u32[]{:S(2)}) async-start(f32[4,4,128]{2,1,0:T(4,128)} %scatter_fusion), calls=%async_computation.1 | async-start | bytes 16384 | tf_op jit(solution)/shard_map/all_to_all | solution.py:101
  78.7 2.0 %fusion.13 = f32[8,4,128]{2,1,0:T(4,128)S(1)} fusion(f32[8,4,128,128]{2,3,1,0:T(8,128)} %get-tuple-element.95, f32[8,4,128]{2,1,0:T(4,128)S(1)} %get-tuple-element.94), kind=kLoop, calls=%fused_computation.28 | loop fusion | flops 1568768 | bytes 2129920 | tf_op jit(solution)/shard_map/vmap()/reduce_sum | solution.py:20
  80.7 1.0 copy.82
  81.7 1.2 copy.84
  83.8 2.5 %scatter_fusion.1 = f32[4,128,256]{2,1,0:T(8,128)} fusion(f32[4,128,256]{2,1,0:T(8,128)} %broadcast_in_dim.95, s32[4]{0:T(128)S(1)} %fusion.45, f32[4,128,256]{2,1,0:T(8,128)S(1)} %copy.84), kind=kCustom, calls=%fused_computation.1 | custom fusion | bytes 1572880 | tf_op jit(solution)/shard_map/scatter | solution.py:92
  86.3 4.5 %all-to-all-start.2 = ((f32[4,128,256]{2,1,0:T(8,128)}), f32[4,128,256]{2,1,0:T(8,128)}, u32[]{:S(2)}, u32[]{:S(2)}) async-start(f32[4,128,256]{2,1,0:T(8,128)} %scatter_fusion.1), calls=%async_computation.2 | async-start | bytes 1048576 | tf_op jit(solution)/shard_map/all_to_all | solution.py:100
  92.2 1.2 fusion.21
  93.6 11.1 %all-to-all-done.2 = f32[4,128,256]{2,1,0:T(8,128)} async-done(((f32[4,128,256]{2,1,0:T(8,128)}), f32[4,128,256]{2,1,0:T(8,128)}, u32[]{:S(2)}, u32[]{:S(2)}) %all-to-all-start.2) | async-done | bytes 524320 | tf_op jit(solution)/shard_map/all_to_all | solution.py:100
  104.7 1.2 copy.85
  106.0 1.4 copy.90
  107.4 7.3 %fusion.22 = f32[128,4,64,8]{2,3,1,0:T(8,128)} fusion(f32[4,128,4,64]{3,0,2,1:T(4,128)} %copy.90, f32[8,4,128]{0,1,2:T(4,128)S(1)} %copy.89, f32[4,4,128]{0,1,2:T(4,128)S(1)} %copy.80, pred[4,8]{1,0:T(4,128)(4,1)S(1)} %get-tuple-element.92), kind=kOutput, calls=%fused_computation.41 | convolution fusion | flops 12632064 | bytes 1597472 | tf_op jit(solution)/shard_map/jfhl,jlhd->flhd/dot_general | solution.py:109
  114.7 3.7 %copy.91 = f32[128,4,64,8]{0,2,1,3:T(8,128)} copy(f32[128,4,64,8]{2,3,1,0:T(8,128)} %fusion.22) | data formatting | bytes 2097152 | tf_op jit(solution)/shard_map/jfhl,jlhd->flhd/dot_general | solution.py:109
  118.4 3.3 %fusion.18 = bf16[8,128,4,64]{1,3,2,0:T(8,128)(2,1)} fusion(bf16[8,128,4,64]{1,3,2,0:T(8,128)(2,1)S(1)} %bitcast.179, f32[8,4,128,128]{2,3,1,0:T(8,128)} %get-tuple-element.95, f32[128,4,64,8]{0,2,1,3:T(8,128)} %copy.91, f32[8,4,128]{2,1,0:T(4,128)S(1)} %get-tuple-element.94, f32[8,128,4]{1,2,0:T(4,128)S(1)} %get-tuple-element.61, ...), kind=kOutput, calls=%fused_computation.37 | convolution fusion | flops 69992448 | bytes 4259840 | tf_op jit(solution)/shard_map/vmap(hqk,khd->qhd)/dot_general | solution.py:21
  121.7 1.4 copy.93
  123.2 2.6 %fusion.27 = f32[1024,1024]{1,0:T(8,128)} fusion(bf16[256,1024]{1,0:T(8,128)(2,1)S(1)} %copy-done.1, bf16[8,128,256]{2,0,1:T(8,128)(2,1)S(1)} %copy.93), kind=kOutput, calls=%fused_computation.45 | convolution fusion | flops 536870912 | bytes 5242880 | tf_op jit(solution)/shard_map/dot_general | solution.py:123
  125.9 44.6 %reduce-scatter.2.cloned.1.call-done = f32[256,1024]{1,0:T(8,128)} async-done(((f32[1024,1024]{1,0:T(8,128)}), f32[256,1024]{1,0:T(8,128)}) %reduce-scatter.2.cloned.1.call-update) | async-done | bytes 1048592 | tf_op jit(solution)/shard_map/reduce_scatter | solution.py:124
  170.4 1.3 convert_bitcast_fusion
  171.7 1.1 copy.111
  (74 shorter events, 11.5 us)
Async XLA Ops:
  6.5 13.2 %copy-start = (bf16[8,128,1024]{2,1,0:T(8,128)(2,1)S(1)}, bf16[8,128,1024]{2,1,0:T(8,128)(2,1)}, u32[]{:S(2)}) copy-start(bf16[8,128,1024]{2,1,0:T(8,128)(2,1)} %param.6) | copy-start | bytes 6291460
  29.6 4.8 %copy-start.5 = (s32[2,2]{1,0:T(2,128)S(1)}, s32[2,2]{1,0:T(2,128)}, u32[]{:S(2)}) copy-start(s32[2,2]{1,0:T(2,128)} %param.9) | copy-start | bytes 52
  30.9 23.0 %all-to-all-start = ((bf16[4,128,768]{1,2,0:T(8,128)(2,1)}), bf16[4,128,768]{1,2,0:T(8,128)(2,1)S(1)}, u32[]{:S(2)}, u32[]{:S(2)}) async-start(bf16[4,128,768]{1,2,0:T(8,128)(2,1)} %copy.79), calls=%async_computation | async-start | bytes 1572864 | tf_op jit(solution)/shard_map/all_to_all | solution.py:68
  61.5 1.1 copy-start.3
  62.6 0.8 copy-start.4
  71.0 1.1 copy-start.3
  72.2 0.8 copy-start.4
  75.4 10.8 %all-to-all-start.1 = ((f32[4,4,128]{2,1,0:T(4,128)}), f32[4,4,128]{2,1,0:T(4,128)S(1)}, u32[]{:S(2)}, u32[]{:S(2)}) async-start(f32[4,4,128]{2,1,0:T(4,128)} %scatter_fusion), calls=%async_computation.1 | async-start | bytes 16384 | tf_op jit(solution)/shard_map/all_to_all | solution.py:101
  86.3 18.5 %all-to-all-start.2 = ((f32[4,128,256]{2,1,0:T(8,128)}), f32[4,128,256]{2,1,0:T(8,128)}, u32[]{:S(2)}, u32[]{:S(2)}) async-start(f32[4,128,256]{2,1,0:T(8,128)} %scatter_fusion.1), calls=%async_computation.2 | async-start | bytes 1048576 | tf_op jit(solution)/shard_map/all_to_all | solution.py:100
  90.8 79.7 %reduce-scatter.2.cloned.1.call-start = ((), (), s32[]{:S(2)}) async-start(), calls=%async_computation.4 | async-start | bytes 5242880 | tf_op jit(solution)/shard_map/reduce_scatter | solution.py:124
  114.7 3.7 %copy-start.2 = (bf16[8,128,256]{1,2,0:T(8,128)(2,1)S(1)}, bf16[8,128,256]{1,2,0:T(8,128)(2,1)}, u32[]{:S(2)}) copy-start(bf16[8,128,256]{1,2,0:T(8,128)(2,1)} %copy.82) | copy-start | bytes 1572868
  118.4 4.8 %copy-start.1 = (bf16[256,1024]{1,0:T(8,128)(2,1)S(1)}, bf16[256,1024]{1,0:T(8,128)(2,1)}, u32[]{:S(2)}) copy-start(bf16[256,1024]{1,0:T(8,128)(2,1)} %param.8) | copy-start | bytes 1572868
Sparse Core Ops, SparseCore 0:
  126.0 44.4 reduce-scatter.1
where the time goes:
time: 181 us; the launch traced here: 180 us
  waiting for transfers between devices  65 us (36%)
  local copies, waits for them, and re-layouts  36.8 us (20%)
  matrix products  24.6 us (14%)
  between operations  13.6 us (8%)
  loops' own time  11.8 us (7%)
  starting transfers between devices  11.2 us (6%)
  blocking collectives  10.3 us (6%)
  other arithmetic  6.28 us (3%)
    reduce_scatter x1, waiting for transfers between devices, local(): lax.psum_scatter(projected, 'heads', scatter_dimension=0, tiled=True)  44.6 us
    another operation x1, loops' own time, local(): lax.map(one_pair, jnp.arange(slots_here, dtype=jnp.int32))  11.8 us
    all_to_all x1, waiting for transfers between devices, local(): lax.all_to_all(back_out, 'frames', split_axis=0, concat_axis=0, tiled=True)  11.1 us
    all_gather x1, blocking collectives, local(): listing = lax.all_gather(pair_slots, 'frames', axis=0, tiled=True)  10.3 us
    all_to_all x1, waiting for transfers between devices, local(): lax.all_to_all(outgoing, 'frames', split_axis=0, concat_axis=0, tiled=True)  9.29 us
    dot_general x1, matrix products, local(): jnp.einsum('jfhl,jlhd->flhd', far_weight, got_out.reshape(devices, length...  7.34 us
    slice x2, local copies, waits for them, and re-layouts, local(): packed[:, :, breadth:2 * breadth]  4.56 us
    all_to_all x1, starting transfers between devices, local(): lax.all_to_all(back_out, 'frames', split_axis=0, concat_axis=0, tiled=True)  4.5 us
  transfers between devices with their start and end apart: 4, of which 3 were waited for; matrix products, arithmetic and copies ran while one was open for 11% of the time, Pallas kernels for 0%

commit v1 on v0

v1 whole, which is shorter than its diff:
```python
import functools

import jax
import jax.numpy as jnp
from jax import lax
from jax.experimental import pallas as pl
from jax.experimental.pallas import tpu as pltpu
from jax.sharding import PartitionSpec as P

HD = 64
MESH = pl.DeviceIdType.MESH


def repeat(count, body):
    if count <= 8:
        for step in range(count):
            body(step)
    else:

        def step_body(step, carry):
            body(step)
            return carry

        lax.fori_loop(0, count, step_body, 0)


def kernel(
    devices, parts, cap,
    pairs_ref, x_ref, w_ref, wo_ref, out_ref,
    listing, listing_s, q_ref, k_ref, v_ref, send1, recv1, send2, recv2,
    so, sm, sl, po, pm, psum, msend, mrecv, wall,
    list_send, list_recv, local_sem, h1_send, h1_recv, h2_send, h2_recv,
    w_send, w_recv, m_send, m_recv,
):
    me = lax.axis_index("frames")
    part = lax.axis_index("heads")
    frames_here, length, breadth = q_ref.shape
    width = x_ref.shape[1]
    heads = breadth // HD
    share = length // parts

    def frame_peer(step):
        return lax.rem(me + step, devices)

    def head_peer(step):
        return lax.rem(part + step, parts)

    barrier = pltpu.get_barrier_semaphore()

    def greet_frames(step):
        pl.semaphore_signal(
            barrier, inc=1, device_id={"frames": frame_peer(step + 1)}, device_id_type=MESH
        )

    def greet_heads(step):
        pl.semaphore_signal(
            barrier, inc=1, device_id={"heads": head_peer(step + 1)}, device_id_type=MESH
        )

    repeat(devices - 1, greet_frames)
    repeat(parts - 1, greet_heads)
    pl.semaphore_wait(barrier, devices + parts - 2)

    def list_copy(step):
        return pltpu.make_async_remote_copy(
            pairs_ref, listing.at[me], list_send.at[step], list_recv.at[step],
            device_id={"frames": frame_peer(step + 1)}, device_id_type=MESH,
        )

    def hop1(step):
        peer = frame_peer(step + 1)
        return pltpu.make_async_remote_copy(
            send1.at[peer], recv1.at[me], h1_send.at[step], h1_recv.at[step],
            device_id={"frames": peer}, device_id_type=MESH,
        )

    def hop2(step):
        peer = frame_peer(step + 1)
        return pltpu.make_async_remote_copy(
            send2.at[peer], recv2.at[me], h2_send.at[step], h2_recv.at[step],
            device_id={"frames": peer}, device_id_type=MESH,
        )

    def w_copy(step):
        return pltpu.make_async_remote_copy(
            wo_ref, wall.at[part], w_send.at[step], w_recv.at[step],
            device_id={"heads": head_peer(step + 1)}, device_id_type=MESH,
        )

    def m_copy(step):
        peer = head_peer(step + 1)
        return pltpu.make_async_remote_copy(
            msend.at[peer], mrecv.at[part], m_send.at[step], m_recv.at[step],
            device_id={"heads": peer}, device_id_type=MESH,
        )

    repeat(devices - 1, lambda s: list_copy(s).start())
    repeat(parts - 1, lambda s: w_copy(s).start())
    listing[me] = pairs_ref[...]

    per = 256 // length
    chunks = frames_here // per

    def project(which, target):
        def body(i, carry):
            rows = x_ref[pl.ds(pl.multiple_of(i * 256, 256), 256), :]
            made = jnp.dot(
                rows,
                w_ref[:, which * breadth : (which + 1) * breadth],
                preferred_element_type=jnp.float32,
            )
            target[pl.ds(i * per, per)] = made.astype(jnp.bfloat16).reshape(per, length, breadth)
            return carry

        lax.fori_loop(0, chunks, body, 0)

    project(1, k_ref)
    project(2, v_ref)

    repeat(devices - 1, lambda s: list_copy(s).wait())
    to_scalar = pltpu.make_async_copy(listing, listing_s, local_sem)
    to_scalar.start()
    to_scalar.wait()

    def mine(owner):
        low = me * frames_here
        frame = jnp.int32(0)
        live = jnp.int32(-1)
        for entry in range(2 * cap):
            value = listing_s[owner, 0, entry]
            hit = (value >= low) & (value < low + frames_here)
            frame = jnp.where(hit, value - low, frame)
            live = jnp.where(hit, value - low, live)
        return frame, live

    def gather(owner):
        frame, _ = mine(owner)
        send1[owner, 0] = k_ref[frame]
        send1[owner, 1] = v_ref[frame]

    repeat(devices, gather)
    repeat(devices - 1, lambda s: hop1(s).start())
    recv1[me] = send1[me]

    project(0, q_ref)

    lane_head = lax.broadcasted_iota(jnp.int32, (length, breadth), 1) // HD

    def attend(queries, key_rows, values):
        stacked = jnp.concatenate(
            [jnp.where(lane_head == h, queries, jnp.zeros_like(queries)) for h in range(heads)],
            axis=0,
        )
        scores = lax.dot_general(
            stacked, key_rows, (((1,), (1,)), ((), ())), preferred_element_type=jnp.float32
        ) * (HD ** -0.5)
        peak = jnp.max(scores, axis=1, keepdims=True)
        lifted = jnp.exp(scores - peak)
        total = jnp.sum(lifted, axis=1, keepdims=True)
        weighted = jnp.dot(
            lifted.astype(jnp.bfloat16), values, preferred_element_type=jnp.float32
        )

        def pick(array):
            shown = jnp.broadcast_to(array[:length], (length, breadth))
            for h in range(1, heads):
                shown = jnp.where(
                    lane_head == h,
                    jnp.broadcast_to(array[h * length : (h + 1) * length], (length, breadth)),
                    shown,
                )
            return shown

        return pick(weighted), pick(peak), pick(total)

    def self_body(f, carry):
        o, m, l = attend(q_ref[f], k_ref[f], v_ref[f])
        so[f] = o
        sm[f] = m
        sl[f] = l
        return carry

    lax.fori_loop(0, frames_here, self_body, 0)

    repeat(devices - 1, lambda s: hop1(s).wait())

    def relay(dest):
        low = dest * frames_here
        partner = me
        for row in range(cap):
            a = listing_s[me, 0, 2 * row]
            b = listing_s[me, 0, 2 * row + 1]
            hit_a = (a >= low) & (a < low + frames_here)
            hit_b = (b >= low) & (b < low + frames_here)
            partner = jnp.where(hit_a, lax.div(b, jnp.int32(frames_here)), partner)
            partner = jnp.where(hit_b, lax.div(a, jnp.int32(frames_here)), partner)
        send2[dest] = recv1[partner]

    repeat(devices, relay)
    repeat(devices - 1, lambda s: hop2(s).start())
    recv2[me] = send2[me]
    repeat(devices - 1, lambda s: hop2(s).wait())

    def pair_body(owner, carry):
        frame, _ = mine(owner)
        o, m, l = attend(q_ref[frame], recv2[owner, 0], recv2[owner, 1])
        po[owner] = o
        pm[owner] = m
        psum[owner] = l
        return carry

    lax.fori_loop(0, devices, pair_body, 0)

    def merge_body(f, carry):
        def raise_peak(owner, top):
            _, live = mine(owner)
            return jnp.maximum(top, jnp.where(live == f, pm[owner], -jnp.inf))

        top = lax.fori_loop(0, devices, raise_peak, sm[f])
        weight = jnp.exp(sm[f] - top)

        def add(owner, state):
            num, den = state
            _, live = mine(owner)
            w = jnp.where(live == f, jnp.exp(pm[owner] - top), 0.0)
            w = jnp.where(live == f, w, 0.0)
            return num + w * po[owner], den + w * psum[owner]

        num, den = lax.fori_loop(0, devices, add, (weight * so[f], weight * sl[f]))
        merged = (num / den).astype(jnp.bfloat16)
        for h in range(parts):
            msend[h, f] = merged[h * share : (h + 1) * share]
        return carry

    lax.fori_loop(0, frames_here, merge_body, 0)

    repeat(parts - 1, lambda s: m_copy(s).start())
    mrecv[part] = msend[part]
    wall[part] = wo_ref[...]
    repeat(parts - 1, lambda s: w_copy(s).wait())
    repeat(parts - 1, lambda s: m_copy(s).wait())
    total = jnp.zeros((frames_here * share, width), jnp.float32)
    for h in range(parts):
        total = total + jnp.dot(
            mrecv[h].reshape(frames_here * share, breadth),
            wall[h],
            preferred_element_type=jnp.float32,
        )
    out_ref[...] = total.astype(jnp.bfloat16).reshape(frames_here, share, width)


def local(tokens, w_qkv, w_out, pair_slots):
    frames_here, length, width = tokens.shape
    breadth = w_qkv.shape[2]
    devices = lax.axis_size("frames")
    parts = lax.axis_size("heads")
    cap = pair_slots.shape[0]
    share = length // parts
    pairs = jnp.zeros((8, 128), jnp.int32).at[0, : 2 * cap].set(pair_slots.reshape(-1))
    bf, f32 = jnp.bfloat16, jnp.float32
    vm = pl.BlockSpec(memory_space=pltpu.VMEM)
    dma = pltpu.SemaphoreType.DMA
    return pl.pallas_call(
        functools.partial(kernel, devices, parts, cap),
        out_shape=jax.ShapeDtypeStruct((frames_here, share, width), bf),
        in_specs=[vm] * 4,
        out_specs=vm,
        scratch_shapes=[
            pltpu.VMEM((devices, 8, 128), jnp.int32),
            pltpu.SMEM((devices, 8, 128), jnp.int32),
            pltpu.VMEM((frames_here, length, breadth), bf),
            pltpu.VMEM((frames_here, length, breadth), bf),
            pltpu.VMEM((frames_here, length, breadth), bf),
        ]
        + [pltpu.VMEM((devices, 2, length, breadth), bf)] * 4
        + [pltpu.VMEM((frames_here, length, breadth), f32)] * 3
        + [pltpu.VMEM((devices, length, breadth), f32)] * 3
        + [
            pltpu.VMEM((parts, frames_here, share, breadth), bf),
            pltpu.VMEM((parts, frames_here, share, breadth), bf),
            pltpu.VMEM((parts, breadth, width), bf),
            dma((devices - 1,)),
            dma((devices - 1,)),
            dma,
        ]
        + [dma((devices - 1,))] * 4
        + [dma((parts - 1,))] * 4,
        compiler_params=pltpu.CompilerParams(
            collective_id=0, has_side_effects=True, vmem_limit_bytes=56 * 1024 * 1024
        ),
    )(
        pairs,
        tokens.reshape(frames_here * length, width),
        w_qkv.reshape(width, 3 * breadth),
        w_out,
    )


def solution(mesh):
    placed = (
        P(("groups", "frames"), None, None),
        P(None, None, "heads"),
        P("heads", None),
        P(("groups", "frames"), None),
    )
    return jax.shard_map(
        local,
        mesh=mesh,
        in_specs=placed,
        out_specs=P(("groups", "frames"), "heads", None),
        check_vma=False,
    )
```

time: 181 us -> 53.1 us (0.29)
  the two profiles are of different devices: /device:TPU:1 before, /device:TPU:9 now
where the time goes in v1:
time: 53.1 us; the launch traced here: 52.9 us
  Pallas kernels  47 us (89%)
  local copies, waits for them, and re-layouts  5.86 us (11%)
    pallas_call x1, Pallas kernels, local(): pl.pallas_call(functools.partial(kernel, devices, parts, cap), out_shape=...  47 us
    unnamed x4, local copies, waits for them, and re-layouts  3.58 us
    reshape x1, local copies, waits for them, and re-layouts, local(): w_qkv.reshape(width, 3 * breadth)  1.59 us

profile of v1, /device:TPU:9, one launch (start us, length us, event | category | flops | bytes accessed | tf_op | source)
XLA Modules:
  0.0 52.9 jit_solution(17352981338456320801)
XLA Ops:
  0.0 1.7 %copy.6 = bf16[1024,3,256]{0,2,1:T(8,128)(2,1)S(1)} copy(bf16[1024,3,256]{2,0,1:T(8,128)(2,1)} %param.7) | data formatting | bytes 3145728 | tf_op args[1]
  1.7 0.0 copy-start
  1.7 1.6 %copy.7.w_ref = bf16[1024,768]{1,0:T(8,128)(2,1)} copy(bf16[1024,768]{0,1:T(8,128)(2,1)S(1)} %bitcast.2) | data formatting | bytes 3145728 | tf_op jit(solution)/shard_map/reshape | solution.py:294
  3.3 0.0 copy-done
  3.3 0.1 reshape.39
  3.4 0.6 %scatter.4.pairs_ref = s32[8,128]{1,0:T(8,128)} pad(s32[1,4]{1,0:T(1,128)S(1)} %reshape.39, s32[]{:T(128)} %constant.26.clone.1), padding=0_7x0_124 | pad | bytes 4116 | tf_op jit(solution)/shard_map/scatter | solution.py:259
  4.0 47.0 %shard_map.46 = bf16[8,32,1024]{2,1,0:T(8,128)(2,1)} custom-call(s32[8,128]{1,0:T(8,128)} %scatter.4.pairs_ref, bf16[1024,1024]{1,0:T(8,128)(2,1)} %bitcast.3, bf16[1024,768]{1,0:T(8,128)(2,1)} %copy.7.w_ref, bf16[256,1024]{1,0:T(8,128)(2,1)} %wo_ref.1), custom_call_target="tpu_custom_call" | custom-call | tf_op jit(solution)/shard_map/pallas_call | solution.py:263
  51.0 1.9 %copy.9 = bf16[8,32,1024]{2,1,0:T(8,128)(2,1)} copy(bf16[8,32,1024]{2,1,0:T(8,128)(2,1)} %shard_map.46) | data formatting | bytes 1048576
Async XLA Ops:
  1.7 1.6 %copy-start = (s32[2,2]{1,0:T(2,128)S(1)}, s32[2,2]{1,0:T(2,128)}, u32[]{:S(2)}) copy-start(s32[2,2]{1,0:T(2,128)} %param.9) | copy-start | bytes 52

commit v2 on v1

v2 whole, which is shorter than its diff:
```python
import functools

import jax
import jax.numpy as jnp
from jax import lax
from jax.experimental import pallas as pl
from jax.experimental.pallas import tpu as pltpu
from jax.sharding import PartitionSpec as P

HD = 64
MESH = pl.DeviceIdType.MESH


def repeat(count, body):
    if count <= 8:
        for step in range(count):
            body(step)
    else:

        def step_body(step, carry):
            body(step)
            return carry

        lax.fori_loop(0, count, step_body, 0)


def kernel(
    devices, parts, cap, groups_out,
    pairs_ref, x_hbm, w_hbm, wo_hbm, out_ref,
    x_ref, w_ref, slots, listing, listing_s, info, q_ref, k_ref, v_ref,
    send1k, send1v, recv1k, recv1v, send2k, send2v, recv2k, recv2v,
    so, sm, sl, top, po, pm, psum, pe, msend, mrecv, wall,
    x_sem, w_sem, wo_sem, list_send, list_recv, local_sem,
    h1k_send, h1k_recv, h1v_send, h1v_recv, h2k_send, h2k_recv, h2v_send, h2v_recv,
    w_send, w_recv, m_send, m_recv,
):
    me = lax.axis_index("frames")
    part = lax.axis_index("heads")
    frames_here, length, breadth = q_ref.shape
    width = x_ref.shape[1]
    heads = breadth // HD
    share = length // parts
    per = 256 // length
    chunks = frames_here // per
    group = frames_here // groups_out

    def frame_peer(step):
        return lax.rem(me + step + 1, devices)

    def head_peer(step):
        return lax.rem(part + step + 1, parts)

    barrier = pltpu.get_barrier_semaphore()

    def greet_frames(step):
        pl.semaphore_signal(
            barrier, inc=1, device_id={"frames": frame_peer(step)}, device_id_type=MESH
        )

    def greet_heads(step):
        pl.semaphore_signal(
            barrier, inc=1, device_id={"heads": head_peer(step)}, device_id_type=MESH
        )

    repeat(devices - 1, greet_frames)
    repeat(parts - 1, greet_heads)

    def x_copy(i):
        rows = pl.ds(i * 256, 256)
        return pltpu.make_async_copy(x_hbm.at[rows], x_ref.at[rows], x_sem.at[i])

    def w_load(which):
        return pltpu.make_async_copy(w_hbm.at[which], w_ref.at[which], w_sem.at[which])

    wo_load = pltpu.make_async_copy(wo_hbm, wall.at[part], wo_sem)
    w_load(1).start()
    for i in range(chunks):
        x_copy(i).start()
    w_load(2).start()
    w_load(0).start()
    wo_load.start()

    slots[...] = jnp.zeros_like(slots)
    slots[: pairs_ref.shape[0], : pairs_ref.shape[1]] = pairs_ref[...]
    listing[me] = slots[...]

    def toward(source, target, sends, recvs):
        def make(step):
            peer = frame_peer(step)
            return pltpu.make_async_remote_copy(
                source.at[peer], target.at[me], sends.at[step], recvs.at[step],
                device_id={"frames": peer}, device_id_type=MESH,
            )

        return make

    hop1k = toward(send1k, recv1k, h1k_send, h1k_recv)
    hop1v = toward(send1v, recv1v, h1v_send, h1v_recv)
    hop2k = toward(send2k, recv2k, h2k_send, h2k_recv)
    hop2v = toward(send2v, recv2v, h2v_send, h2v_recv)

    def list_copy(step):
        return pltpu.make_async_remote_copy(
            slots, listing.at[me], list_send.at[step], list_recv.at[step],
            device_id={"frames": frame_peer(step)}, device_id_type=MESH,
        )

    pairwise = parts == 4
    near = part + 1 - 2 * lax.rem(part, 2)
    across = lax.rem(part + 2, parts)

    def w_copy(step):
        if pairwise:
            block = across if step == 2 else part
            peer = across if step == 0 else near
        else:
            block = part
            peer = head_peer(step)
        return pltpu.make_async_remote_copy(
            wall.at[block], wall.at[block], w_send.at[step], w_recv.at[step],
            device_id={"heads": peer}, device_id_type=MESH,
        )

    def m_copy(g, step):
        peer = head_peer(step)
        return pltpu.make_async_remote_copy(
            msend.at[g, peer], mrecv.at[g, part], m_send.at[g, step], m_recv.at[g, step],
            device_id={"heads": peer}, device_id_type=MESH,
        )

    def project(which, target, first):
        w_load(which).wait()

        def body(i, carry):
            if first:
                x_copy(i).wait()
            rows = x_ref[pl.ds(pl.multiple_of(i * 256, 256), 256), :]
            made = jnp.dot(rows, w_ref[which], preferred_element_type=jnp.float32)
            target[pl.ds(i * per, per)] = made.astype(jnp.bfloat16).reshape(per, length, breadth)
            return carry

        lax.fori_loop(0, chunks, body, 0)

    project(1, k_ref, True)
    pl.semaphore_wait(barrier, devices + parts - 2)
    repeat(devices - 1, lambda s: list_copy(s).start())
    wo_load.wait()
    for s in range(2 if pairwise else parts - 1):
        w_copy(s).start()
    project(2, v_ref, False)

    repeat(devices - 1, lambda s: list_copy(s).wait())
    to_scalar = pltpu.make_async_copy(listing, listing_s, local_sem)
    to_scalar.start()
    to_scalar.wait()

    def gather(owner):
        low = me * frames_here
        frame = jnp.int32(0)
        live = jnp.int32(-1)
        for entry in range(2 * cap):
            value = listing_s[owner, entry // 2, entry % 2]
            hit = (value >= low) & (value < low + frames_here)
            frame = jnp.where(hit, value - low, frame)
            live = jnp.where(hit, value - low, live)
        info[0, owner] = frame
        info[1, owner] = live
        send1k[owner] = k_ref[frame]
        send1v[owner] = v_ref[frame]

    repeat(devices, gather)
    repeat(devices - 1, lambda s: hop1k(s).start())
    repeat(devices - 1, lambda s: hop1v(s).start())
    recv1k[me] = send1k[me]
    recv1v[me] = send1v[me]

    project(0, q_ref, False)

    lane_head = lax.broadcasted_iota(jnp.int32, (length, breadth), 1) // HD

    def pick(array):
        shown = jnp.broadcast_to(array[:length], (length, breadth))
        for h in range(1, heads):
            shown = jnp.where(
                lane_head == h,
                jnp.broadcast_to(array[h * length : (h + 1) * length], (length, breadth)),
                shown,
            )
        return shown

    def lift(queries, key_rows):
        stacked = jnp.concatenate(
            [jnp.where(lane_head == h, queries, jnp.zeros_like(queries)) for h in range(heads)],
            axis=0,
        )
        scores = lax.dot_general(
            stacked, key_rows, (((1,), (1,)), ((), ())), preferred_element_type=jnp.float32
        ) * (HD ** -0.5)
        peak = jnp.max(scores, axis=1, keepdims=True)
        lifted = jnp.exp(scores - peak)
        total = jnp.sum(lifted, axis=1, keepdims=True)
        return lifted.astype(jnp.bfloat16), pick(peak), pick(total)

    def self_body(f, carry):
        e, m, l = lift(q_ref[f], k_ref[f])
        so[f] = pick(jnp.dot(e, v_ref[f], preferred_element_type=jnp.float32))
        sm[f] = m
        sl[f] = l
        return carry

    half = frames_here // 2
    lax.fori_loop(0, half, self_body, 0)

    def relay(source, target):
        def body(dest):
            low = dest * frames_here
            partner = me
            for row in range(cap):
                a = listing_s[me, row, 0]
                b = listing_s[me, row, 1]
                hit_a = (a >= low) & (a < low + frames_here)
                hit_b = (b >= low) & (b < low + frames_here)
                partner = jnp.where(hit_a, lax.div(b, jnp.int32(frames_here)), partner)
                partner = jnp.where(hit_b, lax.div(a, jnp.int32(frames_here)), partner)
            target[dest] = source[partner]

        return body

    repeat(devices - 1, lambda s: hop1k(s).wait())
    repeat(devices, relay(recv1k, send2k))
    repeat(devices - 1, lambda s: hop2k(s).start())
    recv2k[me] = send2k[me]

    lax.fori_loop(half, frames_here, self_body, 0)

    repeat(devices - 1, lambda s: hop1v(s).wait())
    repeat(devices, relay(recv1v, send2v))
    repeat(devices - 1, lambda s: hop2v(s).start())
    recv2v[me] = send2v[me]
    if pairwise:
        w_copy(0).wait()
        w_copy(2).start()

    def pair_scores(owner):
        e, m, l = lift(q_ref[info[0, owner]], recv2k[owner])
        pe[owner] = e
        pm[owner] = m
        psum[owner] = l

    def source_of(step):
        return lax.rem(me + devices - step - 1, devices)

    def arrived_scores(step):
        hop2k(step).wait()
        pair_scores(source_of(step))

    pair_scores(me)
    repeat(devices - 1, arrived_scores)

    def peak_body(f, carry):
        def raise_peak(owner, peak):
            return jnp.maximum(peak, jnp.where(info[1, owner] == f, pm[owner], -jnp.inf))

        peak = lax.fori_loop(0, devices, raise_peak, sm[f], unroll=devices <= 8)
        top[f] = peak
        weight = jnp.exp(sm[f] - peak)
        sm[f] = weight
        sl[f] = weight * sl[f]
        return carry

    lax.fori_loop(0, frames_here, peak_body, 0)

    def pair_weight(owner):
        live = info[1, owner] >= 0
        weight = jnp.where(live, jnp.exp(pm[owner] - top[info[0, owner]]), 0.0)
        weight = jnp.where(live, weight, 0.0)
        pm[owner] = weight
        psum[owner] = weight * psum[owner]

    repeat(devices, pair_weight)

    def den_body(f, carry):
        def add(owner, den):
            return den + jnp.where(info[1, owner] == f, psum[owner], 0.0)

        den = lax.fori_loop(0, devices, add, sl[f], unroll=devices <= 8)
        inverse = 1.0 / den
        top[f] = inverse
        so[f] = so[f] * (sm[f] * inverse)
        return carry

    lax.fori_loop(0, frames_here, den_body, 0)

    def pair_values(owner):
        made = jnp.dot(pe[owner], recv2v[owner], preferred_element_type=jnp.float32)
        po[owner] = pick(made) * (pm[owner] * top[info[0, owner]])

    def arrived_values(step):
        hop2v(step).wait()
        pair_values(source_of(step))

    pair_values(me)
    repeat(devices - 1, arrived_values)

    for g in range(groups_out):

        def merge_body(i, carry):
            f = g * group + i

            def add(owner, state):
                return state + jnp.where(info[1, owner] == f, po[owner], 0.0)

            merged = lax.fori_loop(0, devices, add, so[f], unroll=devices <= 8)
            merged = merged.astype(jnp.bfloat16)
            for h in range(parts):
                msend[g, h, i] = merged[h * share : (h + 1) * share]
            return carry

        lax.fori_loop(0, group, merge_body, 0)
        for s in range(parts - 1):
            m_copy(g, s).start()
        mrecv[g, part] = msend[g, part]

    for s in range(1 if pairwise else 0, parts - 1):
        w_copy(s).wait()
    for g in range(groups_out):
        for s in range(parts - 1):
            m_copy(g, s).wait()
        total = jnp.zeros((group * share, width), jnp.float32)
        for h in range(parts):
            total = total + jnp.dot(
                mrecv[g, h].reshape(group * share, breadth),
                wall[h],
                preferred_element_type=jnp.float32,
            )
        out_ref[pl.ds(g * group, group)] = total.astype(jnp.bfloat16).reshape(
            group, share, width
        )


def local(tokens, w_qkv, w_out, pair_slots):
    frames_here, length, width = tokens.shape
    breadth = w_qkv.shape[2]
    devices = lax.axis_size("frames")
    parts = lax.axis_size("heads")
    cap = pair_slots.shape[0]
    share = length // parts
    rows = -(-cap // 8) * 8
    groups_out = 2
    group = frames_here // groups_out
    bf, f32 = jnp.bfloat16, jnp.float32
    vm = pl.BlockSpec(memory_space=pltpu.VMEM)
    hbm = pl.BlockSpec(memory_space=pl.ANY)
    dma = pltpu.SemaphoreType.DMA
    frame_bf = pltpu.VMEM((frames_here, length, breadth), bf)
    frame_f = pltpu.VMEM((frames_here, length, breadth), f32)
    slot_bf = pltpu.VMEM((devices, length, breadth), bf)
    slot_f = pltpu.VMEM((devices, length, breadth), f32)
    return pl.pallas_call(
        functools.partial(kernel, devices, parts, cap, groups_out),
        out_shape=jax.ShapeDtypeStruct((frames_here, share, width), bf),
        in_specs=[vm, hbm, hbm, hbm],
        out_specs=vm,
        scratch_shapes=[
            pltpu.VMEM((frames_here * length, width), bf),
            pltpu.VMEM((3, width, breadth), bf),
            pltpu.VMEM((rows, 128), jnp.int32),
            pltpu.VMEM((devices, rows, 128), jnp.int32),
            pltpu.SMEM((devices, rows, 128), jnp.int32),
            pltpu.SMEM((2, devices), jnp.int32),
        ]
        + [frame_bf] * 3
        + [slot_bf] * 8
        + [frame_f] * 4
        + [slot_f] * 3
        + [
            pltpu.VMEM((devices, length * (breadth // HD), length), bf),
            pltpu.VMEM((groups_out, parts, group, share, breadth), bf),
            pltpu.VMEM((groups_out, parts, group, share, breadth), bf),
            pltpu.VMEM((parts, breadth, width), bf),
            dma((frames_here * length // 256,)),
            dma((3,)),
            dma,
            dma((devices - 1,)),
            dma((devices - 1,)),
            dma,
        ]
        + [dma((devices - 1,))] * 8
        + [dma((parts - 1,))] * 2
        + [dma((groups_out, parts - 1))] * 2,
        compiler_params=pltpu.CompilerParams(
            collective_id=0, has_side_effects=True, vmem_limit_bytes=60 * 1024 * 1024
        ),
    )(
        pair_slots,
        tokens.reshape(frames_here * length, width),
        jnp.transpose(w_qkv, (1, 0, 2)),
        w_out,
    )


def solution(mesh):
    placed = (
        P(("groups", "frames"), None, None),
        P(None, None, "heads"),
        P("heads", None),
        P(("groups", "frames"), None),
    )
    return jax.shard_map(
        local,
        mesh=mesh,
        in_specs=placed,
        out_specs=P(("groups", "frames"), "heads", None),
        check_vma=False,
    )
```

time: 53.1 us -> 43.3 us (0.82)
  Pallas kernels: 47 us -> 41.2 us
  local copies, waits for them, and re-layouts: 5.86 us -> 1.87 us
    pallas_call x1, Pallas kernels: 47 us -> 41.2 us  [local(): pl.pallas_call(functools.partial(kernel, devices, parts, cap, groups_out)...]
    unnamed x4 -> x1, local copies, waits for them, and re-layouts: 3.58 us -> 1.87 us
    reshape x1 -> x0, local copies, waits for them, and re-layouts: 1.59 us -> none  [local(): w_qkv.reshape(width, 3 * breadth)]
    scatter x1 -> x0, local copies, waits for them, and re-layouts: 0.6 us -> none  [local(): jnp.zeros((8, 128), jnp.int32).at[0, :2 * cap].set(pair_slots.reshape(-1))]
where the time goes in v2:
time: 43.3 us; the launch traced here: 43.1 us
  Pallas kernels  41.2 us (95%)
  local copies, waits for them, and re-layouts  1.87 us (4%)
    pallas_call x1, Pallas kernels, local(): pl.pallas_call(functools.partial(kernel, devices, parts, cap, groups_out)...  41.2 us
    unnamed x1, local copies, waits for them, and re-layouts  1.87 us

profile of v2, /device:TPU:9, one launch (start us, length us, event | category | flops | bytes accessed | tf_op | source)
XLA Modules:
  0.0 43.1 jit_solution(6671608217900446392)
XLA Ops:
  0.0 41.2 %shard_map.46 = bf16[8,32,1024]{2,1,0:T(8,128)(2,1)} custom-call(s32[2,2]{1,0:T(2,128)} %pairs_ref.1, bf16[1024,1024]{1,0:T(8,128)(2,1)} %bitcast.2, bf16[3,1024,256]{2,1,0:T(8,128)(2,1)} %bitcast.3, bf16[256,1024]{1,0:T(8,128)(2,1)} %wo_hbm.1), custom_call_target="tpu_custom_call" | custom-call | tf_op jit(solution)/shard_map/pallas_call | solution.py:359
  41.2 1.9 %copy.6 = bf16[8,32,1024]{2,1,0:T(8,128)(2,1)} copy(bf16[8,32,1024]{2,1,0:T(8,128)(2,1)} %shard_map.46) | data formatting | bytes 1048576

commit v3 on v2

--- a/solution.py
+++ b/solution.py
@@ -28,16 +28,16 @@
     devices, parts, cap, groups_out,
     pairs_ref, x_hbm, w_hbm, wo_hbm, out_ref,
     x_ref, w_ref, slots, listing, listing_s, info, q_ref, k_ref, v_ref,
-    send1k, send1v, recv1k, recv1v, send2k, send2v, recv2k, recv2v,
-    so, sm, sl, top, po, pm, psum, pe, msend, mrecv, wall,
+    send1, recv1, send2, xs,
+    so, sm, sl, top, po, pm, psum, msend, mrecv, wall,
     x_sem, w_sem, wo_sem, list_send, list_recv, local_sem,
-    h1k_send, h1k_recv, h1v_send, h1v_recv, h2k_send, h2k_recv, h2v_send, h2v_recv,
+    h1_send, h1_recv, h2_send, h2_recv, g_send, g_recv,
     w_send, w_recv, m_send, m_recv,
 ):
     me = lax.axis_index("frames")
     part = lax.axis_index("heads")
     frames_here, length, breadth = q_ref.shape
-    width = x_ref.shape[1]
+    width = x_ref.shape[2]
     heads = breadth // HD
     share = length // parts
     per = 256 // length
@@ -66,7 +66,7 @@
     repeat(parts - 1, greet_heads)
 
     def x_copy(i):
-        rows = pl.ds(i * 256, 256)
+        rows = pl.ds(i * per, per)
         return pltpu.make_async_copy(x_hbm.at[rows], x_ref.at[rows], x_sem.at[i])
 
     def w_load(which):
@@ -84,20 +84,22 @@
     slots[: pairs_ref.shape[0], : pairs_ref.shape[1]] = pairs_ref[...]
     listing[me] = slots[...]
 
-    def toward(source, target, sends, recvs):
-        def make(step):
-            peer = frame_peer(step)
-            return pltpu.make_async_remote_copy(
-                source.at[peer], target.at[me], sends.at[step], recvs.at[step],
-                device_id={"frames": peer}, device_id_type=MESH,
-            )
-
-        return make
-
-    hop1k = toward(send1k, recv1k, h1k_send, h1k_recv)
-    hop1v = toward(send1v, recv1v, h1v_send, h1v_recv)
-    hop2k = toward(send2k, recv2k, h2k_send, h2k_recv)
-    hop2v = toward(send2v, recv2v, h2v_send, h2v_recv)
+    def own_rows(block):
+        return pl.ds(pl.multiple_of(block * share, share), share)
+
+    def hop1(step):
+        peer = frame_peer(step)
+        return pltpu.make_async_remote_copy(
+            send1.at[peer], recv1.at[me], h1_send.at[step], h1_recv.at[step],
+            device_id={"frames": peer}, device_id_type=MESH,
+        )
+
+    def hop2(step):
+        peer = frame_peer(step)
+        return pltpu.make_async_remote_copy(
+            send2.at[peer], xs.at[me, own_rows(part)], h2_send.at[step], h2_recv.at[step],
+            device_id={"frames": peer}, device_id_type=MESH,
+        )
 
     def list_copy(step):
         return pltpu.make_async_remote_copy(
@@ -121,6 +123,35 @@
             device_id={"heads": peer}, device_id_type=MESH,
         )
 
+    def slot_of(k):
+        return lax.rem(me + devices - k, devices)
+
+    def g_copy(k, step):
+        if pairwise:
+            block = across if step == 2 else part
+            peer = across if step == 0 else near
+        else:
+            block = part
+            peer = head_peer(step)
+        piece = xs.at[slot_of(k), own_rows(block)]
+        return pltpu.make_async_remote_copy(
+            piece, piece, g_send.at[k, step], g_recv.at[k, step],
+            device_id={"heads": peer}, device_id_type=MESH,
+        )
+
+    def spread(k):
+        for step in range(2 if pairwise else parts - 1):
+            g_copy(k, step).start()
+
+    def forward(k):
+        if pairwise:
+            g_copy(k, 0).wait()
+            g_copy(k, 2).start()
+
+    def collect(k):
+        for step in range(1 if pairwise else 0, parts - 1):
+            g_copy(k, step).wait()
+
     def m_copy(g, step):
         peer = head_peer(step)
         return pltpu.make_async_remote_copy(
@@ -134,7 +165,7 @@
         def body(i, carry):
             if first:
                 x_copy(i).wait()
-            rows = x_ref[pl.ds(pl.multiple_of(i * 256, 256), 256), :]
+            rows = x_ref[pl.ds(i * per, per)].reshape(per * length, width)
             made = jnp.dot(rows, w_ref[which], preferred_element_type=jnp.float32)
             target[pl.ds(i * per, per)] = made.astype(jnp.bfloat16).reshape(per, length, breadth)
             return carry
@@ -147,8 +178,6 @@
     wo_load.wait()
     for s in range(2 if pairwise else parts - 1):
         w_copy(s).start()
-    project(2, v_ref, False)
-
     repeat(devices - 1, lambda s: list_copy(s).wait())
     to_scalar = pltpu.make_async_copy(listing, listing_s, local_sem)
     to_scalar.start()
@@ -165,15 +194,13 @@
             live = jnp.where(hit, value - low, live)
         info[0, owner] = frame
         info[1, owner] = live
-        send1k[owner] = k_ref[frame]
-        send1v[owner] = v_ref[frame]
+        send1[owner] = x_ref[frame, own_rows(part)]
 
     repeat(devices, gather)
-    repeat(devices - 1, lambda s: hop1k(s).start())
-    repeat(devices - 1, lambda s: hop1v(s).start())
-    recv1k[me] = send1k[me]
-    recv1v[me] = send1v[me]
-
+    repeat(devices - 1, lambda s: hop1(s).start())
+    recv1[me] = send1[me]
+
+    project(2, v_ref, False)
     project(0, q_ref, False)
 
     lane_head = lax.broadcasted_iota(jnp.int32, (length, breadth), 1) // HD
@@ -211,51 +238,50 @@
     half = frames_here // 2
     lax.fori_loop(0, half, self_body, 0)
 
-    def relay(source, target):
-        def body(dest):
-            low = dest * frames_here
-            partner = me
-            for row in range(cap):
-                a = listing_s[me, row, 0]
-                b = listing_s[me, row, 1]
-                hit_a = (a >= low) & (a < low + frames_here)
-                hit_b = (b >= low) & (b < low + frames_here)
-                partner = jnp.where(hit_a, lax.div(b, jnp.int32(frames_here)), partner)
-                partner = jnp.where(hit_b, lax.div(a, jnp.int32(frames_here)), partner)
-            target[dest] = source[partner]
-
-        return body
-
-    repeat(devices - 1, lambda s: hop1k(s).wait())
-    repeat(devices, relay(recv1k, send2k))
-    repeat(devices - 1, lambda s: hop2k(s).start())
-    recv2k[me] = send2k[me]
-
-    lax.fori_loop(half, frames_here, self_body, 0)
-
-    repeat(devices - 1, lambda s: hop1v(s).wait())
-    repeat(devices, relay(recv1v, send2v))
-    repeat(devices - 1, lambda s: hop2v(s).start())
-    recv2v[me] = send2v[me]
+    def relay(dest):
+        low = dest * frames_here
+        partner = me
+        for row in range(cap):
+            a = listing_s[me, row, 0]
+            b = listing_s[me, row, 1]
+            hit_a = (a >= low) & (a < low + frames_here)
+            hit_b = (b >= low) & (b < low + frames_here)
+            partner = jnp.where(hit_a, lax.div(b, jnp.int32(frames_here)), partner)
+            partner = jnp.where(hit_b, lax.div(a, jnp.int32(frames_here)), partner)
+        send2[dest] = recv1[partner]
+
+    repeat(devices - 1, lambda s: hop1(s).wait())
+    repeat(devices, relay)
+    repeat(devices - 1, lambda s: hop2(s).start())
+    xs[me, own_rows(part)] = send2[me]
+    spread(0)
     if pairwise:
         w_copy(0).wait()
         w_copy(2).start()
 
-    def pair_scores(owner):
-        e, m, l = lift(q_ref[info[0, owner]], recv2k[owner])
-        pe[owner] = e
+    lax.fori_loop(half, frames_here, self_body, 0)
+    forward(0)
+
+    def pair_attend(k):
+        owner = slot_of(k)
+        rows = xs[owner]
+        keys = jnp.dot(rows, w_ref[1], preferred_element_type=jnp.float32).astype(jnp.bfloat16)
+        values = jnp.dot(rows, w_ref[2], preferred_element_type=jnp.float32).astype(jnp.bfloat16)
+        e, m, l = lift(q_ref[info[0, owner]], keys)
+        po[owner] = pick(jnp.dot(e, values, preferred_element_type=jnp.float32))
         pm[owner] = m
         psum[owner] = l
 
-    def source_of(step):
-        return lax.rem(me + devices - step - 1, devices)
-
-    def arrived_scores(step):
-        hop2k(step).wait()
-        pair_scores(source_of(step))
-
-    pair_scores(me)
-    repeat(devices - 1, arrived_scores)
+    def arrived(step):
+        hop2(step).wait()
+        spread(step + 1)
+        collect(step)
+        pair_attend(step)
+        forward(step + 1)
+
+    repeat(devices - 1, arrived)
+    collect(devices - 1)
+    pair_attend(devices - 1)
 
     def peak_body(f, carry):
         def raise_peak(owner, peak):
@@ -291,16 +317,10 @@
 
     lax.fori_loop(0, frames_here, den_body, 0)
 
-    def pair_values(owner):
-        made = jnp.dot(pe[owner], recv2v[owner], preferred_element_type=jnp.float32)
-        po[owner] = pick(made) * (pm[owner] * top[info[0, owner]])
-
-    def arrived_values(step):
-        hop2v(step).wait()
-        pair_values(source_of(step))
-
-    pair_values(me)
-    repeat(devices - 1, arrived_values)
+    def pair_scale(owner):
+        po[owner] = po[owner] * (pm[owner] * top[info[0, owner]])
+
+    repeat(devices, pair_scale)
 
     for g in range(groups_out):
 
@@ -354,7 +374,7 @@
     dma = pltpu.SemaphoreType.DMA
     frame_bf = pltpu.VMEM((frames_here, length, breadth), bf)
     frame_f = pltpu.VMEM((frames_here, length, breadth), f32)
-    slot_bf = pltpu.VMEM((devices, length, breadth), bf)
+    slot_bf = pltpu.VMEM((devices, share, width), bf)
     slot_f = pltpu.VMEM((devices, length, breadth), f32)
     return pl.pallas_call(
         functools.partial(kernel, devices, parts, cap, groups_out),
@@ -362,7 +382,7 @@
         in_specs=[vm, hbm, hbm, hbm],
         out_specs=vm,
         scratch_shapes=[
-            pltpu.VMEM((frames_here * length, width), bf),
+            pltpu.VMEM((frames_here, length, width), bf),
             pltpu.VMEM((3, width, breadth), bf),
             pltpu.VMEM((rows, 128), jnp.int32),
             pltpu.VMEM((devices, rows, 128), jnp.int32),
@@ -370,11 +390,11 @@
             pltpu.SMEM((2, devices), jnp.int32),
         ]
         + [frame_bf] * 3
-        + [slot_bf] * 8
+        + [slot_bf] * 3
+        + [pltpu.VMEM((devices, length, width), bf)]
         + [frame_f] * 4
         + [slot_f] * 3
         + [
-            pltpu.VMEM((devices, length * (breadth // HD), length), bf),
             pltpu.VMEM((groups_out, parts, group, share, breadth), bf),
             pltpu.VMEM((groups_out, parts, group, share, breadth), bf),
             pltpu.VMEM((parts, breadth, width), bf),
@@ -385,7 +405,8 @@
             dma((devices - 1,)),
             dma,
         ]
-        + [dma((devices - 1,))] * 8
+        + [dma((devices - 1,))] * 4
+        + [dma((devices, parts - 1))] * 2
         + [dma((parts - 1,))] * 2
         + [dma((groups_out, parts - 1))] * 2,
         compiler_params=pltpu.CompilerParams(
@@ -393,7 +414,7 @@
         ),
     )(
         pair_slots,
-        tokens.reshape(frames_here * length, width),
+        tokens,
         jnp.transpose(w_qkv, (1, 0, 2)),
         w_out,
     )

time: 43.3 us -> 45.5 us (1.051)
  the two profiles are of different devices: /device:TPU:9 before, /device:TPU:1 now
where the time goes in v3:
time: 45.5 us; the launch traced here: 45.4 us
  Pallas kernels  43.5 us (96%)
  local copies, waits for them, and re-layouts  1.87 us (4%)
    pallas_call x1, Pallas kernels, local(): pl.pallas_call(functools.partial(kernel, devices, parts, cap, groups_out)...  43.5 us
    unnamed x1, local copies, waits for them, and re-layouts  1.87 us

profile of v3, /device:TPU:1, one launch (start us, length us, event | category | flops | bytes accessed | tf_op | source)
XLA Modules:
  0.0 45.4 jit_solution(447006841589629905)
XLA Ops:
  0.0 43.5 %shard_map.46 = bf16[8,32,1024]{2,1,0:T(8,128)(2,1)} custom-call(s32[2,2]{1,0:T(2,128)} %pairs_ref.1, bf16[8,128,1024]{2,1,0:T(8,128)(2,1)} %x_hbm.1, bf16[3,1024,256]{2,1,0:T(8,128)(2,1)} %bitcast.1, bf16[256,1024]{1,0:T(8,128)(2,1)} %wo_hbm.1), custom_call_target="tpu_custom_call" | custom-call | tf_op jit(solution)/shard_map/pallas_call | solution.py:379
  43.5 1.9 %copy.6 = bf16[8,32,1024]{2,1,0:T(8,128)(2,1)} copy(bf16[8,32,1024]{2,1,0:T(8,128)(2,1)} %shard_map.46) | data formatting | bytes 1048576

commit v4 on v3

--- a/solution.py
+++ b/solution.py
@@ -127,12 +127,8 @@
         return lax.rem(me + devices - k, devices)
 
     def g_copy(k, step):
-        if pairwise:
-            block = across if step == 2 else part
-            peer = across if step == 0 else near
-        else:
-            block = part
-            peer = head_peer(step)
+        block = part
+        peer = head_peer(step)
         piece = xs.at[slot_of(k), own_rows(block)]
         return pltpu.make_async_remote_copy(
             piece, piece, g_send.at[k, step], g_recv.at[k, step],
@@ -140,16 +136,11 @@
         )
 
     def spread(k):
-        for step in range(2 if pairwise else parts - 1):
+        for step in range(parts - 1):
             g_copy(k, step).start()
 
-    def forward(k):
-        if pairwise:
-            g_copy(k, 0).wait()
-            g_copy(k, 2).start()
-
     def collect(k):
-        for step in range(1 if pairwise else 0, parts - 1):
+        for step in range(parts - 1):
             g_copy(k, step).wait()
 
     def m_copy(g, step):
@@ -201,8 +192,6 @@
     recv1[me] = send1[me]
 
     project(2, v_ref, False)
-    project(0, q_ref, False)
-
     lane_head = lax.broadcasted_iota(jnp.int32, (length, breadth), 1) // HD
 
     def pick(array):
@@ -234,9 +223,6 @@
         sm[f] = m
         sl[f] = l
         return carry
-
-    half = frames_here // 2
-    lax.fori_loop(0, half, self_body, 0)
 
     def relay(dest):
         low = dest * frames_here
@@ -255,12 +241,7 @@
     repeat(devices - 1, lambda s: hop2(s).start())
     xs[me, own_rows(part)] = send2[me]
     spread(0)
-    if pairwise:
-        w_copy(0).wait()
-        w_copy(2).start()
-
-    lax.fori_loop(half, frames_here, self_body, 0)
-    forward(0)
+    project(0, q_ref, False)
 
     def pair_attend(k):
         owner = slot_of(k)
@@ -275,13 +256,20 @@
     def arrived(step):
         hop2(step).wait()
         spread(step + 1)
-        collect(step)
-        pair_attend(step)
-        forward(step + 1)
+
+    def finish(k):
+        collect(k)
+        pair_attend(k)
 
     repeat(devices - 1, arrived)
-    collect(devices - 1)
-    pair_attend(devices - 1)
+    lax.fori_loop(0, frames_here, self_body, 0)
+
+    finish(0)
+    repeat(devices - 1, lambda s: finish(s + 1))
+
+    if pairwise:
+        w_copy(0).wait()
+        w_copy(2).start()
 
     def peak_body(f, carry):
         def raise_peak(owner, peak):

time: 45.5 us -> 42.3 us (0.930)
  Pallas kernels: 43.5 us -> 40.3 us
    pallas_call x1, Pallas kernels: 43.5 us -> 40.3 us  [local(): pl.pallas_call(functools.partial(kernel, devices, parts, cap, groups_out)...]
where the time goes in v4:
time: 42.3 us; the launch traced here: 42.2 us
  Pallas kernels  40.3 us (95%)
  local copies, waits for them, and re-layouts  1.87 us (4%)
    pallas_call x1, Pallas kernels, local(): pl.pallas_call(functools.partial(kernel, devices, parts, cap, groups_out)...  40.3 us
    unnamed x1, local copies, waits for them, and re-layouts  1.87 us

profile of v4, /device:TPU:1, one launch (start us, length us, event | category | flops | bytes accessed | tf_op | source)
XLA Modules:
  0.0 42.2 jit_solution(2690235780985560599)
XLA Ops:
  0.0 40.3 %shard_map.46 = bf16[8,32,1024]{2,1,0:T(8,128)(2,1)} custom-call(s32[2,2]{1,0:T(2,128)} %pairs_ref.1, bf16[8,128,1024]{2,1,0:T(8,128)(2,1)} %x_hbm.1, bf16[3,1024,256]{2,1,0:T(8,128)(2,1)} %bitcast.1, bf16[256,1024]{1,0:T(8,128)(2,1)} %wo_hbm.1), custom_call_target="tpu_custom_call" | custom-call | tf_op jit(solution)/shard_map/pallas_call | solution.py:367
  40.3 1.9 %copy.6 = bf16[8,32,1024]{2,1,0:T(8,128)(2,1)} copy(bf16[8,32,1024]{2,1,0:T(8,128)(2,1)} %shard_map.46) | data formatting | bytes 1048576

commit v5 on v4

--- a/solution.py
+++ b/solution.py
@@ -264,12 +264,12 @@
     repeat(devices - 1, arrived)
     lax.fori_loop(0, frames_here, self_body, 0)
 
-    finish(0)
-    repeat(devices - 1, lambda s: finish(s + 1))
-
     if pairwise:
         w_copy(0).wait()
         w_copy(2).start()
+    finish(0)
+    repeat(devices - 1, lambda s: finish(s + 1))
+
 
     def peak_body(f, carry):
         def raise_peak(owner, peak):

time: 42.3 us -> 42.3 us (level)
  no operation moved by 1% of the time
where the time goes in v5:
time: 42.3 us; the launch traced here: 42.2 us
  Pallas kernels  40.3 us (95%)
  local copies, waits for them, and re-layouts  1.87 us (4%)
    pallas_call x1, Pallas kernels, local(): pl.pallas_call(functools.partial(kernel, devices, parts, cap, groups_out)...  40.3 us
    unnamed x1, local copies, waits for them, and re-layouts  1.87 us

profile of v5, /device:TPU:1, one launch (start us, length us, event | category | flops | bytes accessed | tf_op | source)
XLA Modules:
  0.0 42.2 jit_solution(17074545189492978417)
XLA Ops:
  0.0 40.3 %shard_map.46 = bf16[8,32,1024]{2,1,0:T(8,128)(2,1)} custom-call(s32[2,2]{1,0:T(2,128)} %pairs_ref.1, bf16[8,128,1024]{2,1,0:T(8,128)(2,1)} %x_hbm.1, bf16[3,1024,256]{2,1,0:T(8,128)(2,1)} %bitcast.1, bf16[256,1024]{1,0:T(8,128)(2,1)} %wo_hbm.1), custom_call_target="tpu_custom_call" | custom-call | tf_op jit(solution)/shard_map/pallas_call | solution.py:367
  40.3 1.9 %copy.6 = bf16[8,32,1024]{2,1,0:T(8,128)(2,1)} copy(bf16[8,32,1024]{2,1,0:T(8,128)(2,1)} %shard_map.46) | data formatting | bytes 1048576
